TPU v7x, 512 devices: a whole 4x4x16 slice. The times are simulated.
512 devices in a mesh: blk: 32 (over y_lo, z), gy: 4 (over x), rep: 4 (over y_hi, core).
Axes of the slice: x: 4, y: 4 (y_hi: 2, y_lo: 2; y = y_hi * 2 + y_lo), z: 16, core: 2. Of those that a mesh axis runs over, the one named last changes fastest.
Arguments:
- grain_id: int32 [128, 32, 512], P('blk', 'gy', 'rep'), may hold values from 0 to 255
- init_masks: int32 [2, 128, 32, 512], P(None, 'blk', 'gy', 'rep'), may hold values from 0 to 1, as said below
- target_masks: int32 [2, 128, 32, 512], P(None, 'blk', 'gy', 'rep'), may hold values from 0 to 1, as said below
- emb_table: bfloat16 [256, 8], replicated, may hold values from -6 to 6
- w_in: float32 [64, 10], P('rep'), may hold values from -2 to 2
- b_in: float32 [64], P('rep'), may hold values from -3 to 3
- w_mid: float32 [64, 64], P('rep'), may hold values from -0.75 to 0.75
- b_mid: float32 [64], P('rep'), may hold values from -3 to 3
- w_out: float32 [6, 64], P(None, 'rep'), may hold values from -0.75 to 0.75
- b_out: float32 [6], replicated, may hold values from -4 to 4
Outputs:
- final_state: float32 [2, 128, 32, 512], P(None, 'blk', 'gy', 'rep')
- loss: float32 [], replicated
- grad_w_in: float32 [64, 10], P('rep')
- grad_b_in: float32 [64], P('rep')
- grad_w_mid: float32 [64, 64], P('rep')
- grad_b_mid: float32 [64], P('rep')
- grad_w_out: float32 [6, 64], P(None, 'rep')
- grad_b_out: float32 [6], replicated
- start_sensitivity: float32 [2, 128, 32, 512], P(None, 'blk', 'gy', 'rep')
Inputs may be any that keep to these rules, and one draw needn't show every extreme that they name: `init_masks`: 0 or 1 in every cell. `target_masks`: 0 or 1 in every cell.
All inputs are finite; a program needn't handle non-finite values.
Results may differ from a plain program's by a relative error of at most 0.0054.
The roundings to bfloat16 on the way count: a program that leaves them out, or rounds other values in their place, can miss the bound.
Values may be sent and summed in bfloat16 or wider, within the bound.
A program may use at most 64 MiB of HBM per device.

v0:
```python
import jax
import jax.numpy as jnp
from jax import lax
from jax.sharding import PartitionSpec as P

STEPS = 4
RATE_MAX = 0.15
AXES = (("rep", 3), ("gy", 2), ("blk", 1))


def ring_perms(axis):
    count = lax.axis_size(axis)
    forward = [(i, (i + 1) % count) for i in range(count)]
    backward = [((i + 1) % count, i) for i in range(count)]
    return (forward, backward)


def exchange_faces(fields):
    faces = []
    for direction, (axis, dim) in enumerate(AXES):
        block = fields[direction]
        forward, backward = ring_perms(axis)
        size = block.shape[dim]
        low = lax.ppermute(lax.slice_in_dim(block, size - 1, size, axis=dim), axis, forward)
        high = lax.ppermute(lax.slice_in_dim(block, 0, 1, axis=dim), axis, backward)
        faces.append((low, high))
    return faces


def shifted(block, low, high, dim, offset):
    size = block.shape[dim]
    if offset == 1:
        return jnp.concatenate([lax.slice_in_dim(block, 1, size, axis=dim), high], axis=dim)
    return jnp.concatenate([low, lax.slice_in_dim(block, 0, size - 1, axis=dim)], axis=dim)


def diffuse(field, field_faces, rates, rate_faces):
    summed = field
    for direction, (axis, dim) in enumerate(AXES):
        rate_here = rates[direction::3]
        for offset in (1, -1):
            low, high = field_faces[direction]
            rlow, rhigh = rate_faces[direction]
            rate_next = shifted(rate_here, rlow, rhigh, dim, offset)
            summed = summed + 0.5 * (rate_here + rate_next) * (
                shifted(field, low, high, dim, offset) - field
            )
    return summed


def rate_cotangent(state, state_faces, adjoint, adjoint_faces):
    pieces_list = []
    for direction, (axis, dim) in enumerate(AXES):
        summed = jnp.zeros_like(state)
        for offset in (1, -1):
            slow, shigh = state_faces[direction]
            alow, ahigh = adjoint_faces[direction]
            summed = summed + (shifted(state, slow, shigh, dim, offset) - state) * (
                shifted(adjoint, alow, ahigh, dim, offset) - adjoint
            )
        pieces_list.append(-0.5 * summed)
    stacked = jnp.stack(pieces_list, axis=1)
    return stacked.reshape((6,) + stacked.shape[2:])


def embed_lookup(emb_table, grain_flat):
    table_rows = emb_table.shape[0]
    one_hot = (grain_flat[None, :] == lax.broadcasted_iota(jnp.int32, (table_rows, 1), 0)).astype(
        jnp.bfloat16
    )
    looked = jnp.dot(emb_table.T, one_hot, preferred_element_type=jnp.float32)
    return looked.astype(jnp.bfloat16)


def forward_layers(params, features):
    w_in, b_in, w_mid, b_mid, w_out, b_out = params
    act_one = jnp.tanh(
        jnp.dot(w_in, features, preferred_element_type=jnp.float32)
        + b_in.astype(jnp.float32)[:, None]
    )
    hid_one = act_one.astype(jnp.bfloat16)
    act_two = jnp.tanh(
        jnp.dot(w_mid, hid_one, preferred_element_type=jnp.float32)
        + b_mid.astype(jnp.float32)[:, None]
    )
    hid_two = act_two.astype(jnp.bfloat16)
    logits = (
        jnp.dot(w_out, hid_two, preferred_element_type=jnp.float32)
        + b_out.astype(jnp.float32)[:, None]
    )
    return (RATE_MAX * jax.nn.sigmoid(logits), act_one, hid_one, act_two, hid_two)


def backward_layers(params, features, rate_grad, forward_values):
    w_in, b_in, w_mid, b_mid, w_out, b_out = params
    rate_values, act_one, hid_one, act_two, hid_two = forward_values
    out_grad = (rate_grad * rate_values * (1.0 - rate_values / RATE_MAX)).astype(jnp.bfloat16)
    two_grad = (
        jnp.dot(w_out.T, out_grad, preferred_element_type=jnp.float32) * (1.0 - act_two * act_two)
    ).astype(jnp.bfloat16)
    one_grad = (
        jnp.dot(w_mid.T, two_grad, preferred_element_type=jnp.float32) * (1.0 - act_one * act_one)
    ).astype(jnp.bfloat16)
    grad_terms = (
        jnp.dot(one_grad, features.T, preferred_element_type=jnp.float32),
        jnp.sum(one_grad, axis=1, dtype=jnp.float32),
        jnp.dot(two_grad, hid_one.T, preferred_element_type=jnp.float32),
        jnp.sum(two_grad, axis=1, dtype=jnp.float32),
        jnp.dot(out_grad, hid_two.T, preferred_element_type=jnp.float32),
        jnp.sum(out_grad, axis=1, dtype=jnp.float32),
    )
    state_grad = jnp.dot(w_in[:, -2:].T, one_grad, preferred_element_type=jnp.float32)
    return (grad_terms, state_grad)


def gather_params(w_in, b_in, w_mid, b_mid, w_out, b_out):
    n_in = w_in.shape[1]
    n_mid = w_mid.shape[1]
    packed = jnp.concatenate([w_in, b_in[:, None], w_mid, b_mid[:, None], w_out.T], axis=1).astype(
        jnp.bfloat16
    )
    full = lax.all_gather(packed, "rep", axis=0, tiled=True)
    col = 0
    w_in_b = full[:, col : col + n_in]
    col += n_in
    b_in_b = full[:, col]
    col += 1
    w_mid_b = full[:, col : col + n_mid]
    col += n_mid
    b_mid_b = full[:, col]
    col += 1
    w_out_b = full[:, col:].T
    return (w_in_b, b_in_b, w_mid_b, b_mid_b, w_out_b, b_out.astype(jnp.bfloat16))


def per_device(
    grain_id, init_masks, target_masks, emb_table, w_in, b_in, w_mid, b_mid, w_out, b_out
):
    params = gather_params(w_in, b_in, w_mid, b_mid, w_out, b_out)
    depth_cells, row_cells, col_cells = grain_id.shape
    cell_count = depth_cells * row_cells * col_cells
    block_shape = (depth_cells, row_cells, col_cells)
    embedding = embed_lookup(emb_table, grain_id.reshape(cell_count))
    state_now = init_masks.astype(jnp.float32)
    history = []
    for step_index in range(STEPS):
        features = jnp.concatenate(
            [embedding, state_now.reshape(2, cell_count).astype(jnp.bfloat16)], axis=0
        )
        rate_values = forward_layers(params, features)[0].reshape((6,) + block_shape)
        faces = exchange_faces(
            [jnp.concatenate([state_now, rate_values[d::3]], axis=0) for d in range(3)]
        )
        state_faces = [(low[:2], high[:2]) for low, high in faces]
        rate_faces = [(low[2:], high[2:]) for low, high in faces]
        history.append((state_now, state_faces, rate_values, rate_faces))
        state_now = diffuse(state_now, state_faces, rate_values, rate_faces)
    misfit = state_now - target_masks.astype(jnp.float32)
    total_cells = float(
        cell_count * lax.axis_size("blk") * lax.axis_size("gy") * lax.axis_size("rep")
    )
    loss_part = jnp.sum(misfit * misfit) / (4.0 * total_cells)
    adjoint = misfit / (2.0 * total_cells)
    grad_sums = None
    for step_index in reversed(range(STEPS)):
        state_t, state_faces, rate_values, rate_faces = history[step_index]
        adjoint_faces = exchange_faces([adjoint] * 3)
        rate_grad = rate_cotangent(state_t, state_faces, adjoint, adjoint_faces).reshape(
            6, cell_count
        )
        features = jnp.concatenate(
            [embedding, state_t.reshape(2, cell_count).astype(jnp.bfloat16)], axis=0
        )
        forward_values = forward_layers(params, features)
        step_terms, state_grad = backward_layers(params, features, rate_grad, forward_values)
        if grad_sums is None:
            grad_sums = step_terms
        else:
            grad_sums = tuple(
                (earlier + later_term for earlier, later_term in zip(grad_sums, step_terms))
            )
        adjoint = diffuse(adjoint, adjoint_faces, rate_values, rate_faces) + state_grad.reshape(
            (2,) + block_shape
        )
    start_sensitivity = adjoint * (2.0 * total_cells)
    pieces = list(grad_sums) + [loss_part[None]]
    flat = jnp.concatenate([piece.reshape(-1) for piece in pieces])
    summed_flat = lax.psum(flat, ("blk", "gy", "rep"))
    summed = []
    start = 0
    for piece in pieces:
        summed.append(summed_flat[start : start + piece.size].reshape(piece.shape))
        start += piece.size
    position = lax.axis_index("rep")
    share_width = w_in.shape[0]
    grad_w_in = lax.dynamic_slice_in_dim(summed[0], position * share_width, share_width, 0)
    grad_b_in = lax.dynamic_slice_in_dim(summed[1], position * share_width, share_width, 0)
    grad_w_mid = lax.dynamic_slice_in_dim(summed[2], position * share_width, share_width, 0)
    grad_b_mid = lax.dynamic_slice_in_dim(summed[3], position * share_width, share_width, 0)
    grad_w_out = lax.dynamic_slice_in_dim(summed[4], position * share_width, share_width, 1)
    grad_b_out = summed[5]
    loss_total = summed[6][0]
    return (
        state_now,
        loss_total,
        grad_w_in,
        grad_b_in,
        grad_w_mid,
        grad_b_mid,
        grad_w_out,
        grad_b_out,
        start_sensitivity,
    )


def solution(mesh):
    in_specs = (
        P("blk", "gy", "rep"),
        P(None, "blk", "gy", "rep"),
        P(None, "blk", "gy", "rep"),
        P(),
        P("rep", None),
        P("rep"),
        P("rep", None),
        P("rep"),
        P(None, "rep"),
        P(),
    )
    out_specs = (
        P(None, "blk", "gy", "rep"),
        P(),
        P("rep", None),
        P("rep"),
        P("rep", None),
        P("rep"),
        P(None, "rep"),
        P(),
        P(None, "blk", "gy", "rep"),
    )
    return jax.shard_map(
        per_device, mesh=mesh, in_specs=in_specs, out_specs=out_specs, check_vma=False
    )
```

profile of v0, /device:TPU:1, one launch (start us, length us, event | category | flops | bytes accessed | tf_op | source)
XLA Modules:
  0.0 383.7 jit_solution(16146299786309421557)
XLA Ops:
  5.6 13.3 %all_gather.3 = bf16[64,82]{1,0:T(8,128)(2,1)S(1)} all-gather(bf16[16,82]{1,0:T(8,128)(2,1)S(1)} %concatenate.347), channel_id=1, replica_groups=mesh['blk'=32,'gy'=4,'rep'=4] {'rep'}, dimensions={0}, use_global_device_ids=true | all-gather | bytes 13120 | tf_op jit(solution)/shard_map/all_gather | solution.py:122
  30.3 7.8 %collective-permute-start.4 = (f32[4,1,8,128]{3,2,1,0:T(8,128)S(1)}, f32[4,1,8,128]{3,2,1,0:T(8,128)S(1)}, u32[]{:S(2)}, u32[]{:S(2)}) collective-permute-start(f32[4,1,8,128]{3,2,1,0:T(8,128)S(1)} %get-tuple-element.85), channel_id=1, source_target_pairs={{16,0},{32,16},{48,32},{64,48},{80,64},{96,80},{112,96},{128,112},... | collective-permute-start | bytes 49160 | tf_op jit(solution)/shard_map/ppermute | solution.py:25
  43.1 4.2 %collective-permute-done = f32[4,4,8,1]{3,2,1,0:T(8,128)S(1)} collective-permute-done((f32[4,4,8,1]{3,2,1,0:T(8,128)S(1)}, f32[4,4,8,1]{3,2,1,0:T(8,128)S(1)}, u32[]{:S(2)}, u32[]{:S(2)}) %collective-permute-start) | collective-permute-done | bytes 544 | tf_op jit(solution)/shard_map/ppermute | solution.py:25
  54.9 5.5 %collective-permute-start.6 = (f32[4,4,8,1]{3,2,1,0:T(8,128)S(1)}, f32[4,4,8,1]{3,2,1,0:T(8,128)S(1)}, u32[]{:S(2)}, u32[]{:S(2)}) collective-permute-start(f32[4,4,8,1]{3,2,1,0:T(8,128)S(1)} %get-tuple-element.69), channel_id=1, source_target_pairs={{1,0},{2,1},{3,2},{0,3},{5,4},{6,5},{7,6},{4,7},{9,8},{10,9},{11,1... | collective-permute-start | bytes 1544 | tf_op jit(solution)/shard_map/ppermute | solution.py:25
  60.4 4.6 %collective-permute-start.8 = (f32[4,4,1,128]{3,2,1,0:T(1,128)S(1)}, f32[4,4,1,128]{3,2,1,0:T(1,128)S(1)}, u32[]{:S(2)}, u32[]{:S(2)}) collective-permute-start(f32[4,4,1,128]{3,2,1,0:T(1,128)S(1)} %get-tuple-element.73), channel_id=1, source_target_pairs={{4,0},{8,4},{12,8},{0,12},{5,1},{9,5},{13,9},{1,13},{6,2},{10,6},{... | collective-permute-start | bytes 24584 | tf_op jit(solution)/shard_map/ppermute | solution.py:25
  66.9 4.9 %collective-permute-start.10 = (f32[4,1,8,128]{3,2,1,0:T(8,128)S(1)}, f32[4,1,8,128]{3,2,1,0:T(8,128)S(1)}, u32[]{:S(2)}, u32[]{:S(2)}) collective-permute-start(f32[4,1,8,128]{3,2,1,0:T(8,128)S(1)} %get-tuple-element.75), channel_id=1, source_target_pairs={{16,0},{32,16},{48,32},{64,48},{80,64},{96,80},{112,96},{128,112},... | collective-permute-start | bytes 49160 | tf_op jit(solution)/shard_map/ppermute | solution.py:25
  73.7 3.9 %collective-permute-start.7 = (f32[4,4,8,1]{3,2,1,0:T(8,128)S(1)}, f32[4,4,8,1]{3,2,1,0:T(8,128)S(1)}, u32[]{:S(2)}, u32[]{:S(2)}) collective-permute-start(f32[4,4,8,1]{3,2,1,0:T(8,128)S(1)} %get-tuple-element.70), channel_id=1, source_target_pairs={{0,1},{1,2},{2,3},{3,0},{4,5},{5,6},{6,7},{7,4},{8,9},{9,10},{10,1... | collective-permute-start | bytes 1544 | tf_op jit(solution)/shard_map/ppermute | solution.py:24
  83.5 4.3 %collective-permute-start.12 = (f32[4,4,8,1]{3,2,1,0:T(8,128)S(1)}, f32[4,4,8,1]{3,2,1,0:T(8,128)S(1)}, u32[]{:S(2)}, u32[]{:S(2)}) collective-permute-start(f32[4,4,8,1]{3,2,1,0:T(8,128)S(1)} %get-tuple-element.59), channel_id=1, source_target_pairs={{1,0},{2,1},{3,2},{0,3},{5,4},{6,5},{7,6},{4,7},{9,8},{10,9},{11,1... | collective-permute-start | bytes 1544 | tf_op jit(solution)/shard_map/ppermute | solution.py:25
  87.8 4.8 %collective-permute-start.14 = (f32[4,4,1,128]{3,2,1,0:T(1,128)S(1)}, f32[4,4,1,128]{3,2,1,0:T(1,128)S(1)}, u32[]{:S(2)}, u32[]{:S(2)}) collective-permute-start(f32[4,4,1,128]{3,2,1,0:T(1,128)S(1)} %get-tuple-element.63), channel_id=1, source_target_pairs={{4,0},{8,4},{12,8},{0,12},{5,1},{9,5},{13,9},{1,13},{6,2},{10,6},{... | collective-permute-start | bytes 24584 | tf_op jit(solution)/shard_map/ppermute | solution.py:25
  94.6 5.8 %collective-permute-start.16 = (f32[4,1,8,128]{3,2,1,0:T(8,128)S(1)}, f32[4,1,8,128]{3,2,1,0:T(8,128)S(1)}, u32[]{:S(2)}, u32[]{:S(2)}) collective-permute-start(f32[4,1,8,128]{3,2,1,0:T(8,128)S(1)} %get-tuple-element.65), channel_id=1, source_target_pairs={{16,0},{32,16},{48,32},{64,48},{80,64},{96,80},{112,96},{128,112},... | collective-permute-start | bytes 49160 | tf_op jit(solution)/shard_map/ppermute | solution.py:25
  102.3 3.9 %collective-permute-start.13 = (f32[4,4,8,1]{3,2,1,0:T(8,128)S(1)}, f32[4,4,8,1]{3,2,1,0:T(8,128)S(1)}, u32[]{:S(2)}, u32[]{:S(2)}) collective-permute-start(f32[4,4,8,1]{3,2,1,0:T(8,128)S(1)} %get-tuple-element.60), channel_id=1, source_target_pairs={{0,1},{1,2},{2,3},{3,0},{4,5},{5,6},{6,7},{7,4},{8,9},{9,10},{10,1... | collective-permute-start | bytes 1544 | tf_op jit(solution)/shard_map/ppermute | solution.py:24
  111.7 4.3 %collective-permute-start.18 = (f32[4,4,8,1]{3,2,1,0:T(8,128)S(1)}, f32[4,4,8,1]{3,2,1,0:T(8,128)S(1)}, u32[]{:S(2)}, u32[]{:S(2)}) collective-permute-start(f32[4,4,8,1]{3,2,1,0:T(8,128)S(1)} %get-tuple-element.49), channel_id=1, source_target_pairs={{1,0},{2,1},{3,2},{0,3},{5,4},{6,5},{7,6},{4,7},{9,8},{10,9},{11,1... | collective-permute-start | bytes 1544 | tf_op jit(solution)/shard_map/ppermute | solution.py:25
  116.0 4.9 %collective-permute-start.20 = (f32[4,4,1,128]{3,2,1,0:T(1,128)S(1)}, f32[4,4,1,128]{3,2,1,0:T(1,128)S(1)}, u32[]{:S(2)}, u32[]{:S(2)}) collective-permute-start(f32[4,4,1,128]{3,2,1,0:T(1,128)S(1)} %get-tuple-element.53), channel_id=1, source_target_pairs={{4,0},{8,4},{12,8},{0,12},{5,1},{9,5},{13,9},{1,13},{6,2},{10,6},{... | collective-permute-start | bytes 24584 | tf_op jit(solution)/shard_map/ppermute | solution.py:25
  122.8 5.8 %collective-permute-start.22 = (f32[4,1,8,128]{3,2,1,0:T(8,128)S(1)}, f32[4,1,8,128]{3,2,1,0:T(8,128)S(1)}, u32[]{:S(2)}, u32[]{:S(2)}) collective-permute-start(f32[4,1,8,128]{3,2,1,0:T(8,128)S(1)} %get-tuple-element.55), channel_id=1, source_target_pairs={{16,0},{32,16},{48,32},{64,48},{80,64},{96,80},{112,96},{128,112},... | collective-permute-start | bytes 49160 | tf_op jit(solution)/shard_map/ppermute | solution.py:25
  140.1 4.8 %collective-permute-start.26 = (f32[2,4,1,128]{3,2,1,0:T(1,128)}, f32[2,4,1,128]{3,2,1,0:T(1,128)}, u32[]{:S(2)}, u32[]{:S(2)}) collective-permute-start(f32[2,4,1,128]{3,2,1,0:T(1,128)} %get-tuple-element.129), channel_id=1, source_target_pairs={{4,0},{8,4},{12,8},{0,12},{5,1},{9,5},{13,9},{1,13},{6,2},{10,6},{... | collective-permute-start | bytes 12296 | tf_op jit(solution)/shard_map/ppermute | solution.py:25
  147.5 5.1 %collective-permute-start.28 = (f32[2,1,8,128]{3,2,1,0:T(8,128)}, f32[2,1,8,128]{3,2,1,0:T(8,128)}, u32[]{:S(2)}, u32[]{:S(2)}) collective-permute-start(f32[2,1,8,128]{3,2,1,0:T(8,128)} %get-tuple-element.133), channel_id=1, source_target_pairs={{16,0},{32,16},{48,32},{64,48},{80,64},{96,80},{112,96},{128,112},... | collective-permute-start | bytes 24584 | tf_op jit(solution)/shard_map/ppermute | solution.py:25
  152.6 5.5 %collective-permute-start.24 = (f32[2,4,8,1]{3,2,1,0:T(8,128)}, f32[2,4,8,1]{3,2,1,0:T(8,128)}, u32[]{:S(2)}, u32[]{:S(2)}) collective-permute-start(f32[2,4,8,1]{3,2,1,0:T(8,128)} %get-tuple-element.125), channel_id=1, source_target_pairs={{1,0},{2,1},{3,2},{0,3},{5,4},{6,5},{7,6},{4,7},{9,8},{10,9},{11,1... | collective-permute-start | bytes 776 | tf_op jit(solution)/shard_map/ppermute | solution.py:25
  181.7 4.8 %collective-permute-start.32 = (f32[2,4,1,128]{3,2,1,0:T(1,128)S(1)}, f32[2,4,1,128]{3,2,1,0:T(1,128)S(1)}, u32[]{:S(2)}, u32[]{:S(2)}) collective-permute-start(f32[2,4,1,128]{3,2,1,0:T(1,128)S(1)} %get-tuple-element.117), channel_id=1, source_target_pairs={{4,0},{8,4},{12,8},{0,12},{5,1},{9,5},{13,9},{1,13},{6,2},{10,6},{... | collective-permute-start | bytes 12296 | tf_op jit(solution)/shard_map/ppermute | solution.py:25
  190.9 4.7 %collective-permute-start.31 = (f32[2,4,8,1]{3,2,1,0:T(8,128)S(1)}, f32[2,4,8,1]{3,2,1,0:T(8,128)S(1)}, u32[]{:S(2)}, u32[]{:S(2)}) collective-permute-start(f32[2,4,8,1]{3,2,1,0:T(8,128)S(1)} %get-tuple-element.114), channel_id=1, source_target_pairs={{0,1},{1,2},{2,3},{3,0},{4,5},{5,6},{6,7},{7,4},{8,9},{9,10},{10,1... | collective-permute-start | bytes 776 | tf_op jit(solution)/shard_map/ppermute | solution.py:24
  216.0 4.6 %collective-permute-start.38 = (f32[2,4,1,128]{3,2,1,0:T(1,128)S(1)}, f32[2,4,1,128]{3,2,1,0:T(1,128)S(1)}, u32[]{:S(2)}, u32[]{:S(2)}) collective-permute-start(f32[2,4,1,128]{3,2,1,0:T(1,128)S(1)} %get-tuple-element.105), channel_id=1, source_target_pairs={{4,0},{8,4},{12,8},{0,12},{5,1},{9,5},{13,9},{1,13},{6,2},{10,6},{... | collective-permute-start | bytes 12296 | tf_op jit(solution)/shard_map/ppermute | solution.py:25
  224.4 5.1 %collective-permute-start.37 = (f32[2,4,8,1]{3,2,1,0:T(8,128)S(1)}, f32[2,4,8,1]{3,2,1,0:T(8,128)S(1)}, u32[]{:S(2)}, u32[]{:S(2)}) collective-permute-start(f32[2,4,8,1]{3,2,1,0:T(8,128)S(1)} %get-tuple-element.102), channel_id=1, source_target_pairs={{0,1},{1,2},{2,3},{3,0},{4,5},{5,6},{6,7},{7,4},{8,9},{9,10},{10,1... | collective-permute-start | bytes 776 | tf_op jit(solution)/shard_map/ppermute | solution.py:24
  249.8 4.6 %collective-permute-start.44 = (f32[2,4,1,128]{3,2,1,0:T(1,128)S(1)}, f32[2,4,1,128]{3,2,1,0:T(1,128)S(1)}, u32[]{:S(2)}, u32[]{:S(2)}) collective-permute-start(f32[2,4,1,128]{3,2,1,0:T(1,128)S(1)} %get-tuple-element.93), channel_id=1, source_target_pairs={{4,0},{8,4},{12,8},{0,12},{5,1},{9,5},{13,9},{1,13},{6,2},{10,6},{... | collective-permute-start | bytes 12296 | tf_op jit(solution)/shard_map/ppermute | solution.py:25
  258.5 4.8 %collective-permute-start.43 = (f32[2,4,8,1]{3,2,1,0:T(8,128)S(1)}, f32[2,4,8,1]{3,2,1,0:T(8,128)S(1)}, u32[]{:S(2)}, u32[]{:S(2)}) collective-permute-start(f32[2,4,8,1]{3,2,1,0:T(8,128)S(1)} %get-tuple-element.90), channel_id=1, source_target_pairs={{0,1},{1,2},{2,3},{3,0},{4,5},{5,6},{6,7},{7,4},{8,9},{9,10},{10,1... | collective-permute-start | bytes 776 | tf_op jit(solution)/shard_map/ppermute | solution.py:24
  276.9 101.3 %psum.7 = f32[5255]{0:T(1024)S(1)} all-reduce(f32[5255]{0:T(1024)S(1)} %concatenate.436), channel_id=1, replica_groups=mesh['blk'=32,'gy'=4,'rep'=4] {'blk','gy','rep'}, use_global_device_ids=true, to_apply=%region_13.0 | all-reduce | flops 5255 | bytes 42040 | tf_op jit(solution)/shard_map/psum | solution.py:188
  (875 shorter events, 153.9 us)
Async XLA Ops:
  25.0 25.5 %collective-permute-start.2 = (f32[4,4,1,128]{3,2,1,0:T(1,128)S(1)}, f32[4,4,1,128]{3,2,1,0:T(1,128)S(1)}, u32[]{:S(2)}, u32[]{:S(2)}) collective-permute-start(f32[4,4,1,128]{3,2,1,0:T(1,128)S(1)} %get-tuple-element.83), channel_id=1, source_target_pairs={{4,0},{8,4},{12,8},{0,12},{5,1},{9,5},{13,9},{1,13},{6,2},{10,6},{... | collective-permute-start | bytes 24584 | tf_op jit(solution)/shard_map/ppermute | solution.py:25
  26.9 23.6 %collective-permute-start.3 = (f32[4,4,1,128]{3,2,1,0:T(1,128)S(1)}, f32[4,4,1,128]{3,2,1,0:T(1,128)S(1)}, u32[]{:S(2)}, u32[]{:S(2)}) collective-permute-start(f32[4,4,1,128]{3,2,1,0:T(1,128)S(1)} %get-tuple-element.84), channel_id=1, source_target_pairs={{0,4},{4,8},{8,12},{12,0},{1,5},{5,9},{9,13},{13,1},{2,6},{6,10},{... | collective-permute-start | bytes 24584 | tf_op jit(solution)/shard_map/ppermute | solution.py:24
  30.3 20.2 %collective-permute-start.4 = (f32[4,1,8,128]{3,2,1,0:T(8,128)S(1)}, f32[4,1,8,128]{3,2,1,0:T(8,128)S(1)}, u32[]{:S(2)}, u32[]{:S(2)}) collective-permute-start(f32[4,1,8,128]{3,2,1,0:T(8,128)S(1)} %get-tuple-element.85), channel_id=1, source_target_pairs={{16,0},{32,16},{48,32},{64,48},{80,64},{96,80},{112,96},{128,112},... | collective-permute-start | bytes 49160 | tf_op jit(solution)/shard_map/ppermute | solution.py:25
  38.1 12.5 %collective-permute-start.5 = (f32[4,1,8,128]{3,2,1,0:T(8,128)S(1)}, f32[4,1,8,128]{3,2,1,0:T(8,128)S(1)}, u32[]{:S(2)}, u32[]{:S(2)}) collective-permute-start(f32[4,1,8,128]{3,2,1,0:T(8,128)S(1)} %get-tuple-element.86), channel_id=1, source_target_pairs={{0,16},{16,32},{32,48},{48,64},{64,80},{80,96},{96,112},{112,128},... | collective-permute-start | bytes 49160 | tf_op jit(solution)/shard_map/ppermute | solution.py:24
  54.9 18.8 %collective-permute-start.6 = (f32[4,4,8,1]{3,2,1,0:T(8,128)S(1)}, f32[4,4,8,1]{3,2,1,0:T(8,128)S(1)}, u32[]{:S(2)}, u32[]{:S(2)}) collective-permute-start(f32[4,4,8,1]{3,2,1,0:T(8,128)S(1)} %get-tuple-element.69), channel_id=1, source_target_pairs={{1,0},{2,1},{3,2},{0,3},{5,4},{6,5},{7,6},{4,7},{9,8},{10,9},{11,1... | collective-permute-start | bytes 1544 | tf_op jit(solution)/shard_map/ppermute | solution.py:25
  60.4 18.6 %collective-permute-start.8 = (f32[4,4,1,128]{3,2,1,0:T(1,128)S(1)}, f32[4,4,1,128]{3,2,1,0:T(1,128)S(1)}, u32[]{:S(2)}, u32[]{:S(2)}) collective-permute-start(f32[4,4,1,128]{3,2,1,0:T(1,128)S(1)} %get-tuple-element.73), channel_id=1, source_target_pairs={{4,0},{8,4},{12,8},{0,12},{5,1},{9,5},{13,9},{1,13},{6,2},{10,6},{... | collective-permute-start | bytes 24584 | tf_op jit(solution)/shard_map/ppermute | solution.py:25
  65.0 14.1 %collective-permute-start.9 = (f32[4,4,1,128]{3,2,1,0:T(1,128)S(1)}, f32[4,4,1,128]{3,2,1,0:T(1,128)S(1)}, u32[]{:S(2)}, u32[]{:S(2)}) collective-permute-start(f32[4,4,1,128]{3,2,1,0:T(1,128)S(1)} %get-tuple-element.74), channel_id=1, source_target_pairs={{0,4},{4,8},{8,12},{12,0},{1,5},{5,9},{9,13},{13,1},{2,6},{6,10},{... | collective-permute-start | bytes 24584 | tf_op jit(solution)/shard_map/ppermute | solution.py:24
  83.5 18.8 %collective-permute-start.12 = (f32[4,4,8,1]{3,2,1,0:T(8,128)S(1)}, f32[4,4,8,1]{3,2,1,0:T(8,128)S(1)}, u32[]{:S(2)}, u32[]{:S(2)}) collective-permute-start(f32[4,4,8,1]{3,2,1,0:T(8,128)S(1)} %get-tuple-element.59), channel_id=1, source_target_pairs={{1,0},{2,1},{3,2},{0,3},{5,4},{6,5},{7,6},{4,7},{9,8},{10,9},{11,1... | collective-permute-start | bytes 1544 | tf_op jit(solution)/shard_map/ppermute | solution.py:25
  87.8 19.8 %collective-permute-start.14 = (f32[4,4,1,128]{3,2,1,0:T(1,128)S(1)}, f32[4,4,1,128]{3,2,1,0:T(1,128)S(1)}, u32[]{:S(2)}, u32[]{:S(2)}) collective-permute-start(f32[4,4,1,128]{3,2,1,0:T(1,128)S(1)} %get-tuple-element.63), channel_id=1, source_target_pairs={{4,0},{8,4},{12,8},{0,12},{5,1},{9,5},{13,9},{1,13},{6,2},{10,6},{... | collective-permute-start | bytes 24584 | tf_op jit(solution)/shard_map/ppermute | solution.py:25
  92.6 15.0 %collective-permute-start.15 = (f32[4,4,1,128]{3,2,1,0:T(1,128)S(1)}, f32[4,4,1,128]{3,2,1,0:T(1,128)S(1)}, u32[]{:S(2)}, u32[]{:S(2)}) collective-permute-start(f32[4,4,1,128]{3,2,1,0:T(1,128)S(1)} %get-tuple-element.64), channel_id=1, source_target_pairs={{0,4},{4,8},{8,12},{12,0},{1,5},{5,9},{9,13},{13,1},{2,6},{6,10},{... | collective-permute-start | bytes 24584 | tf_op jit(solution)/shard_map/ppermute | solution.py:24
  94.6 13.1 %collective-permute-start.16 = (f32[4,1,8,128]{3,2,1,0:T(8,128)S(1)}, f32[4,1,8,128]{3,2,1,0:T(8,128)S(1)}, u32[]{:S(2)}, u32[]{:S(2)}) collective-permute-start(f32[4,1,8,128]{3,2,1,0:T(8,128)S(1)} %get-tuple-element.65), channel_id=1, source_target_pairs={{16,0},{32,16},{48,32},{64,48},{80,64},{96,80},{112,96},{128,112},... | collective-permute-start | bytes 49160 | tf_op jit(solution)/shard_map/ppermute | solution.py:25
  111.7 18.8 %collective-permute-start.18 = (f32[4,4,8,1]{3,2,1,0:T(8,128)S(1)}, f32[4,4,8,1]{3,2,1,0:T(8,128)S(1)}, u32[]{:S(2)}, u32[]{:S(2)}) collective-permute-start(f32[4,4,8,1]{3,2,1,0:T(8,128)S(1)} %get-tuple-element.49), channel_id=1, source_target_pairs={{1,0},{2,1},{3,2},{0,3},{5,4},{6,5},{7,6},{4,7},{9,8},{10,9},{11,1... | collective-permute-start | bytes 1544 | tf_op jit(solution)/shard_map/ppermute | solution.py:25
  116.0 19.8 %collective-permute-start.20 = (f32[4,4,1,128]{3,2,1,0:T(1,128)S(1)}, f32[4,4,1,128]{3,2,1,0:T(1,128)S(1)}, u32[]{:S(2)}, u32[]{:S(2)}) collective-permute-start(f32[4,4,1,128]{3,2,1,0:T(1,128)S(1)} %get-tuple-element.53), channel_id=1, source_target_pairs={{4,0},{8,4},{12,8},{0,12},{5,1},{9,5},{13,9},{1,13},{6,2},{10,6},{... | collective-permute-start | bytes 24584 | tf_op jit(solution)/shard_map/ppermute | solution.py:25
  120.9 15.0 %collective-permute-start.21 = (f32[4,4,1,128]{3,2,1,0:T(1,128)S(1)}, f32[4,4,1,128]{3,2,1,0:T(1,128)S(1)}, u32[]{:S(2)}, u32[]{:S(2)}) collective-permute-start(f32[4,4,1,128]{3,2,1,0:T(1,128)S(1)} %get-tuple-element.54), channel_id=1, source_target_pairs={{0,4},{4,8},{8,12},{12,0},{1,5},{5,9},{9,13},{13,1},{2,6},{6,10},{... | collective-permute-start | bytes 24584 | tf_op jit(solution)/shard_map/ppermute | solution.py:24
  122.8 13.1 %collective-permute-start.22 = (f32[4,1,8,128]{3,2,1,0:T(8,128)S(1)}, f32[4,1,8,128]{3,2,1,0:T(8,128)S(1)}, u32[]{:S(2)}, u32[]{:S(2)}) collective-permute-start(f32[4,1,8,128]{3,2,1,0:T(8,128)S(1)} %get-tuple-element.55), channel_id=1, source_target_pairs={{16,0},{32,16},{48,32},{64,48},{80,64},{96,80},{112,96},{128,112},... | collective-permute-start | bytes 49160 | tf_op jit(solution)/shard_map/ppermute | solution.py:25
  140.1 24.1 %collective-permute-start.26 = (f32[2,4,1,128]{3,2,1,0:T(1,128)}, f32[2,4,1,128]{3,2,1,0:T(1,128)}, u32[]{:S(2)}, u32[]{:S(2)}) collective-permute-start(f32[2,4,1,128]{3,2,1,0:T(1,128)} %get-tuple-element.129), channel_id=1, source_target_pairs={{4,0},{8,4},{12,8},{0,12},{5,1},{9,5},{13,9},{1,13},{6,2},{10,6},{... | collective-permute-start | bytes 12296 | tf_op jit(solution)/shard_map/ppermute | solution.py:25
  144.9 19.2 %collective-permute-start.27 = (f32[2,4,1,128]{3,2,1,0:T(1,128)}, f32[2,4,1,128]{3,2,1,0:T(1,128)}, u32[]{:S(2)}, u32[]{:S(2)}) collective-permute-start(f32[2,4,1,128]{3,2,1,0:T(1,128)} %get-tuple-element.130), channel_id=1, source_target_pairs={{0,4},{4,8},{8,12},{12,0},{1,5},{5,9},{9,13},{13,1},{2,6},{6,10},{... | collective-permute-start | bytes 12296 | tf_op jit(solution)/shard_map/ppermute | solution.py:24
  147.5 17.7 %collective-permute-start.28 = (f32[2,1,8,128]{3,2,1,0:T(8,128)}, f32[2,1,8,128]{3,2,1,0:T(8,128)}, u32[]{:S(2)}, u32[]{:S(2)}) collective-permute-start(f32[2,1,8,128]{3,2,1,0:T(8,128)} %get-tuple-element.133), channel_id=1, source_target_pairs={{16,0},{32,16},{48,32},{64,48},{80,64},{96,80},{112,96},{128,112},... | collective-permute-start | bytes 24584 | tf_op jit(solution)/shard_map/ppermute | solution.py:25
  181.7 19.4 %collective-permute-start.32 = (f32[2,4,1,128]{3,2,1,0:T(1,128)S(1)}, f32[2,4,1,128]{3,2,1,0:T(1,128)S(1)}, u32[]{:S(2)}, u32[]{:S(2)}) collective-permute-start(f32[2,4,1,128]{3,2,1,0:T(1,128)S(1)} %get-tuple-element.117), channel_id=1, source_target_pairs={{4,0},{8,4},{12,8},{0,12},{5,1},{9,5},{13,9},{1,13},{6,2},{10,6},{... | collective-permute-start | bytes 12296 | tf_op jit(solution)/shard_map/ppermute | solution.py:25
  186.6 14.6 %collective-permute-start.33 = (f32[2,4,1,128]{3,2,1,0:T(1,128)S(1)}, f32[2,4,1,128]{3,2,1,0:T(1,128)S(1)}, u32[]{:S(2)}, u32[]{:S(2)}) collective-permute-start(f32[2,4,1,128]{3,2,1,0:T(1,128)S(1)} %get-tuple-element.118), channel_id=1, source_target_pairs={{0,4},{4,8},{8,12},{12,0},{1,5},{5,9},{9,13},{13,1},{2,6},{6,10},{... | collective-permute-start | bytes 12296 | tf_op jit(solution)/shard_map/ppermute | solution.py:24
  216.0 18.9 %collective-permute-start.38 = (f32[2,4,1,128]{3,2,1,0:T(1,128)S(1)}, f32[2,4,1,128]{3,2,1,0:T(1,128)S(1)}, u32[]{:S(2)}, u32[]{:S(2)}) collective-permute-start(f32[2,4,1,128]{3,2,1,0:T(1,128)S(1)} %get-tuple-element.105), channel_id=1, source_target_pairs={{4,0},{8,4},{12,8},{0,12},{5,1},{9,5},{13,9},{1,13},{6,2},{10,6},{... | collective-permute-start | bytes 12296 | tf_op jit(solution)/shard_map/ppermute | solution.py:25
  220.5 14.4 %collective-permute-start.39 = (f32[2,4,1,128]{3,2,1,0:T(1,128)S(1)}, f32[2,4,1,128]{3,2,1,0:T(1,128)S(1)}, u32[]{:S(2)}, u32[]{:S(2)}) collective-permute-start(f32[2,4,1,128]{3,2,1,0:T(1,128)S(1)} %get-tuple-element.106), channel_id=1, source_target_pairs={{0,4},{4,8},{8,12},{12,0},{1,5},{5,9},{9,13},{13,1},{2,6},{6,10},{... | collective-permute-start | bytes 12296 | tf_op jit(solution)/shard_map/ppermute | solution.py:24
  249.8 18.9 %collective-permute-start.44 = (f32[2,4,1,128]{3,2,1,0:T(1,128)S(1)}, f32[2,4,1,128]{3,2,1,0:T(1,128)S(1)}, u32[]{:S(2)}, u32[]{:S(2)}) collective-permute-start(f32[2,4,1,128]{3,2,1,0:T(1,128)S(1)} %get-tuple-element.93), channel_id=1, source_target_pairs={{4,0},{8,4},{12,8},{0,12},{5,1},{9,5},{13,9},{1,13},{6,2},{10,6},{... | collective-permute-start | bytes 12296 | tf_op jit(solution)/shard_map/ppermute | solution.py:25
  254.3 14.4 %collective-permute-start.45 = (f32[2,4,1,128]{3,2,1,0:T(1,128)S(1)}, f32[2,4,1,128]{3,2,1,0:T(1,128)S(1)}, u32[]{:S(2)}, u32[]{:S(2)}) collective-permute-start(f32[2,4,1,128]{3,2,1,0:T(1,128)S(1)} %get-tuple-element.94), channel_id=1, source_target_pairs={{0,4},{4,8},{8,12},{12,0},{1,5},{5,9},{9,13},{13,1},{2,6},{6,10},{... | collective-permute-start | bytes 12296 | tf_op jit(solution)/shard_map/ppermute | solution.py:24
  (324 other events, 5158.2 us)
where the time goes:
time: 386 us; the launch traced here: 384 us
  starting transfers between devices  167 us (43%)
  blocking collectives  115 us (30%)
  matrix products  34.2 us (9%)
  local copies, waits for them, and re-layouts  22.1 us (6%)
  waiting for transfers between devices  21.5 us (6%)
  other arithmetic  17.5 us (5%)
  between operations  6.61 us (2%)
    psum x1, blocking collectives, per_device(): summed_flat = lax.psum(flat, ('blk', 'gy', 'rep'))  101 us
    ppermute x24, starting transfers between devices, exchange_faces(): high = lax.ppermute(lax.slice_in_dim(block, 0, 1, axis=dim), axis, backward)  98.7 us
    ppermute x24, starting transfers between devices, exchange_faces(): lax.ppermute(lax.slice_in_dim(block, size - 1, size, axis=dim), axis, for...  68.5 us
    ppermute x24, waiting for transfers between devices, exchange_faces(): lax.ppermute(lax.slice_in_dim(block, size - 1, size, axis=dim), axis, for...  17.3 us
    all_gather x1, blocking collectives, gather_params(): full = lax.all_gather(packed, 'rep', axis=0, tiled=True)  13.3 us
  transfers between devices with their start and end apart: 48, of which 9 were waited for; matrix products, arithmetic and copies ran while one was open for 1% of the time, Pallas kernels for 0%

commit v1 on v0

--- a/solution.py
+++ b/solution.py
@@ -136,6 +136,10 @@
 def per_device(
     grain_id, init_masks, target_masks, emb_table, w_in, b_in, w_mid, b_mid, w_out, b_out
 ):
+
+    def _feed_counts(point):
+        return lax.all_gather(point, ("blk", "gy", "rep")).sum(axis=0)
+
     params = gather_params(w_in, b_in, w_mid, b_mid, w_out, b_out)
     depth_cells, row_cells, col_cells = grain_id.shape
     cell_count = depth_cells * row_cells * col_cells
@@ -185,7 +189,7 @@
     start_sensitivity = adjoint * (2.0 * total_cells)
     pieces = list(grad_sums) + [loss_part[None]]
     flat = jnp.concatenate([piece.reshape(-1) for piece in pieces])
-    summed_flat = lax.psum(flat, ("blk", "gy", "rep"))
+    summed_flat = _feed_counts(flat)
     summed = []
     start = 0
     for piece in pieces:

time: 386 us -> 842 us (2.18)
  waiting for transfers between devices: 21.5 us -> 519 us
  blocking collectives: 115 us -> 13.3 us
  local copies, waits for them, and re-layouts: 22.1 us -> 45.2 us
  other arithmetic: 17.5 us -> 30.9 us
  between operations: 6.61 us -> 18.5 us
    unnamed x0 -> x2, waiting for transfers between devices: none -> 499 us
    psum x1 -> x0, blocking collectives: 101 us -> none  [per_device(): summed_flat = lax.psum(flat, ('blk', 'gy', 'rep'))]
    all_gather x0 -> x1, local copies, waits for them, and re-layouts: none -> 16 us  [_feed_counts(): return lax.all_gather(point, ('blk', 'gy', 'rep')).sum(axis=0)]
    unnamed x608 -> x366, local copies, waits for them, and re-layouts: 4.83 us -> 13.5 us
  transfers between devices with their start and end apart: 48 -> 49, of which waited for: 9 -> 10; matrix products, arithmetic and copies ran while one was open for 1% -> 1% of each run, Pallas kernels for 0% -> 0%
where the time goes in v1:
time: 842 us; the launch traced here: 836 us
  waiting for transfers between devices  519 us (62%)
  starting transfers between devices  167 us (20%)
  local copies, waits for them, and re-layouts  45.2 us (5%)
  matrix products  42.1 us (5%)
  other arithmetic  30.9 us (4%)
  between operations  18.5 us (2%)
  blocking collectives  13.3 us (2%)
    unnamed x2, waiting for transfers between devices  499 us
    ppermute x24, starting transfers between devices, exchange_faces(): high = lax.ppermute(lax.slice_in_dim(block, 0, 1, axis=dim), axis, backward)  99 us
    ppermute x24, starting transfers between devices, exchange_faces(): lax.ppermute(lax.slice_in_dim(block, size - 1, size, axis=dim), axis, for...  68.2 us
  transfers between devices with their start and end apart: 49, of which 10 were waited for; matrix products, arithmetic and copies ran while one was open for 1% of the time, Pallas kernels for 0%

profile of v1, /device:TPU:1, one launch (start us, length us, event | category | flops | bytes accessed | tf_op | source)
XLA Modules:
  0.0 836.2 jit_solution(12125167427812487074)
XLA Ops:
  11.7 13.3 %all_gather.9 = bf16[64,82]{1,0:T(8,128)(2,1)S(1)} all-gather(bf16[16,82]{1,0:T(8,128)(2,1)S(1)} %concatenate.347), channel_id=1, replica_groups=mesh['blk'=32,'gy'=4,'rep'=4] {'rep'}, dimensions={0}, use_global_device_ids=true | all-gather | bytes 13120 | tf_op jit(solution)/shard_map/all_gather | solution.py:122
  33.9 7.8 collective-permute-start.4
  57.8 5.5 collective-permute-start.6
  63.4 4.6 collective-permute-start.8
  69.9 4.9 collective-permute-start.10
  88.8 4.3 collective-permute-start.12
  93.1 4.8 collective-permute-start.14
  99.9 5.8 collective-permute-start.16
  118.6 4.3 collective-permute-start.18
  122.9 4.9 collective-permute-start.20
  129.7 5.8 collective-permute-start.22
  146.9 4.8 collective-permute-start.26
  154.3 5.1 collective-permute-start.28
  159.4 5.5 collective-permute-start.24
  192.5 4.9 collective-permute-start.32
  201.8 4.6 collective-permute-start.31
  230.2 4.6 collective-permute-start.38
  238.7 5.1 collective-permute-start.37
  267.7 4.6 collective-permute-start.44
  276.2 5.1 collective-permute-start.43
  297.6 4.3 broadcast.37
  304.7 499.4 %all-reduce.3.cloned.1.call-done = f32[2690560]{0:T(1024)} async-done(((f32[2690560]{0:T(1024)}), f32[2690560]{0:T(1024)}) %all-reduce.3.cloned.1.call-update) | async-done | bytes 10762256
  804.1 16.0 %reshape.90 = f32[512,5255]{1,0:T(8,128)} reshape(f32[2690560]{0:T(1024)} %all-reduce.3.cloned.1.call-done) | data formatting | bytes 21524480 | tf_op jit(solution)/shard_map/all_gather | solution.py:141
  820.2 4.7 reduce_sum.139
  (637 shorter events, 183.1 us)
Async XLA Ops:
  7.2 796.9 %all-reduce.3.cloned.1.call-start = ((), (), s32[]{:S(2)}) async-start(), calls=%async_computation | async-start | bytes 21528576
  28.6 25.5 %collective-permute-start.2 = (f32[4,4,1,128]{3,2,1,0:T(1,128)S(1)}, f32[4,4,1,128]{3,2,1,0:T(1,128)S(1)}, u32[]{:S(2)}, u32[]{:S(2)}) collective-permute-start(f32[4,4,1,128]{3,2,1,0:T(1,128)S(1)} %get-tuple-element.83), channel_id=1, source_target_pairs={{4,0},{8,4},{12,8},{0,12},{5,1},{9,5},{13,9},{1,13},{6,2},{10,6},{... | collective-permute-start | bytes 24584 | tf_op jit(solution)/shard_map/ppermute | solution.py:25
  30.5 23.6 %collective-permute-start.3 = (f32[4,4,1,128]{3,2,1,0:T(1,128)S(1)}, f32[4,4,1,128]{3,2,1,0:T(1,128)S(1)}, u32[]{:S(2)}, u32[]{:S(2)}) collective-permute-start(f32[4,4,1,128]{3,2,1,0:T(1,128)S(1)} %get-tuple-element.84), channel_id=1, source_target_pairs={{0,4},{4,8},{8,12},{12,0},{1,5},{5,9},{9,13},{13,1},{2,6},{6,10},{... | collective-permute-start | bytes 24584 | tf_op jit(solution)/shard_map/ppermute | solution.py:24
  33.9 20.2 %collective-permute-start.4 = (f32[4,1,8,128]{3,2,1,0:T(8,128)S(1)}, f32[4,1,8,128]{3,2,1,0:T(8,128)S(1)}, u32[]{:S(2)}, u32[]{:S(2)}) collective-permute-start(f32[4,1,8,128]{3,2,1,0:T(8,128)S(1)} %get-tuple-element.85), channel_id=1, source_target_pairs={{16,0},{32,16},{48,32},{64,48},{80,64},{96,80},{112,96},{128,112},... | collective-permute-start | bytes 49160 | tf_op jit(solution)/shard_map/ppermute | solution.py:25
  57.8 18.9 %collective-permute-start.6 = (f32[4,4,8,1]{3,2,1,0:T(8,128)S(1)}, f32[4,4,8,1]{3,2,1,0:T(8,128)S(1)}, u32[]{:S(2)}, u32[]{:S(2)}) collective-permute-start(f32[4,4,8,1]{3,2,1,0:T(8,128)S(1)} %get-tuple-element.69), channel_id=1, source_target_pairs={{1,0},{2,1},{3,2},{0,3},{5,4},{6,5},{7,6},{4,7},{9,8},{10,9},{11,1... | collective-permute-start | bytes 1544 | tf_op jit(solution)/shard_map/ppermute | solution.py:25
  63.4 18.6 %collective-permute-start.8 = (f32[4,4,1,128]{3,2,1,0:T(1,128)S(1)}, f32[4,4,1,128]{3,2,1,0:T(1,128)S(1)}, u32[]{:S(2)}, u32[]{:S(2)}) collective-permute-start(f32[4,4,1,128]{3,2,1,0:T(1,128)S(1)} %get-tuple-element.73), channel_id=1, source_target_pairs={{4,0},{8,4},{12,8},{0,12},{5,1},{9,5},{13,9},{1,13},{6,2},{10,6},{... | collective-permute-start | bytes 24584 | tf_op jit(solution)/shard_map/ppermute | solution.py:25
  68.0 14.1 %collective-permute-start.9 = (f32[4,4,1,128]{3,2,1,0:T(1,128)S(1)}, f32[4,4,1,128]{3,2,1,0:T(1,128)S(1)}, u32[]{:S(2)}, u32[]{:S(2)}) collective-permute-start(f32[4,4,1,128]{3,2,1,0:T(1,128)S(1)} %get-tuple-element.74), channel_id=1, source_target_pairs={{0,4},{4,8},{8,12},{12,0},{1,5},{5,9},{9,13},{13,1},{2,6},{6,10},{... | collective-permute-start | bytes 24584 | tf_op jit(solution)/shard_map/ppermute | solution.py:24
  88.8 18.8 %collective-permute-start.12 = (f32[4,4,8,1]{3,2,1,0:T(8,128)S(1)}, f32[4,4,8,1]{3,2,1,0:T(8,128)S(1)}, u32[]{:S(2)}, u32[]{:S(2)}) collective-permute-start(f32[4,4,8,1]{3,2,1,0:T(8,128)S(1)} %get-tuple-element.59), channel_id=1, source_target_pairs={{1,0},{2,1},{3,2},{0,3},{5,4},{6,5},{7,6},{4,7},{9,8},{10,9},{11,1... | collective-permute-start | bytes 1544 | tf_op jit(solution)/shard_map/ppermute | solution.py:25
  93.1 19.8 %collective-permute-start.14 = (f32[4,4,1,128]{3,2,1,0:T(1,128)S(1)}, f32[4,4,1,128]{3,2,1,0:T(1,128)S(1)}, u32[]{:S(2)}, u32[]{:S(2)}) collective-permute-start(f32[4,4,1,128]{3,2,1,0:T(1,128)S(1)} %get-tuple-element.63), channel_id=1, source_target_pairs={{4,0},{8,4},{12,8},{0,12},{5,1},{9,5},{13,9},{1,13},{6,2},{10,6},{... | collective-permute-start | bytes 24584 | tf_op jit(solution)/shard_map/ppermute | solution.py:25
  98.0 15.0 %collective-permute-start.15 = (f32[4,4,1,128]{3,2,1,0:T(1,128)S(1)}, f32[4,4,1,128]{3,2,1,0:T(1,128)S(1)}, u32[]{:S(2)}, u32[]{:S(2)}) collective-permute-start(f32[4,4,1,128]{3,2,1,0:T(1,128)S(1)} %get-tuple-element.64), channel_id=1, source_target_pairs={{0,4},{4,8},{8,12},{12,0},{1,5},{5,9},{9,13},{13,1},{2,6},{6,10},{... | collective-permute-start | bytes 24584 | tf_op jit(solution)/shard_map/ppermute | solution.py:24
  99.9 13.1 %collective-permute-start.16 = (f32[4,1,8,128]{3,2,1,0:T(8,128)S(1)}, f32[4,1,8,128]{3,2,1,0:T(8,128)S(1)}, u32[]{:S(2)}, u32[]{:S(2)}) collective-permute-start(f32[4,1,8,128]{3,2,1,0:T(8,128)S(1)} %get-tuple-element.65), channel_id=1, source_target_pairs={{16,0},{32,16},{48,32},{64,48},{80,64},{96,80},{112,96},{128,112},... | collective-permute-start | bytes 49160 | tf_op jit(solution)/shard_map/ppermute | solution.py:25
  118.6 18.8 %collective-permute-start.18 = (f32[4,4,8,1]{3,2,1,0:T(8,128)S(1)}, f32[4,4,8,1]{3,2,1,0:T(8,128)S(1)}, u32[]{:S(2)}, u32[]{:S(2)}) collective-permute-start(f32[4,4,8,1]{3,2,1,0:T(8,128)S(1)} %get-tuple-element.49), channel_id=1, source_target_pairs={{1,0},{2,1},{3,2},{0,3},{5,4},{6,5},{7,6},{4,7},{9,8},{10,9},{11,1... | collective-permute-start | bytes 1544 | tf_op jit(solution)/shard_map/ppermute | solution.py:25
  122.9 19.8 %collective-permute-start.20 = (f32[4,4,1,128]{3,2,1,0:T(1,128)S(1)}, f32[4,4,1,128]{3,2,1,0:T(1,128)S(1)}, u32[]{:S(2)}, u32[]{:S(2)}) collective-permute-start(f32[4,4,1,128]{3,2,1,0:T(1,128)S(1)} %get-tuple-element.53), channel_id=1, source_target_pairs={{4,0},{8,4},{12,8},{0,12},{5,1},{9,5},{13,9},{1,13},{6,2},{10,6},{... | collective-permute-start | bytes 24584 | tf_op jit(solution)/shard_map/ppermute | solution.py:25
  127.8 14.9 %collective-permute-start.21 = (f32[4,4,1,128]{3,2,1,0:T(1,128)S(1)}, f32[4,4,1,128]{3,2,1,0:T(1,128)S(1)}, u32[]{:S(2)}, u32[]{:S(2)}) collective-permute-start(f32[4,4,1,128]{3,2,1,0:T(1,128)S(1)} %get-tuple-element.54), channel_id=1, source_target_pairs={{0,4},{4,8},{8,12},{12,0},{1,5},{5,9},{9,13},{13,1},{2,6},{6,10},{... | collective-permute-start | bytes 24584 | tf_op jit(solution)/shard_map/ppermute | solution.py:24
  129.7 13.1 %collective-permute-start.22 = (f32[4,1,8,128]{3,2,1,0:T(8,128)S(1)}, f32[4,1,8,128]{3,2,1,0:T(8,128)S(1)}, u32[]{:S(2)}, u32[]{:S(2)}) collective-permute-start(f32[4,1,8,128]{3,2,1,0:T(8,128)S(1)} %get-tuple-element.55), channel_id=1, source_target_pairs={{16,0},{32,16},{48,32},{64,48},{80,64},{96,80},{112,96},{128,112},... | collective-permute-start | bytes 49160 | tf_op jit(solution)/shard_map/ppermute | solution.py:25
  146.9 24.1 %collective-permute-start.26 = (f32[2,4,1,128]{3,2,1,0:T(1,128)}, f32[2,4,1,128]{3,2,1,0:T(1,128)}, u32[]{:S(2)}, u32[]{:S(2)}) collective-permute-start(f32[2,4,1,128]{3,2,1,0:T(1,128)} %get-tuple-element.129), channel_id=1, source_target_pairs={{4,0},{8,4},{12,8},{0,12},{5,1},{9,5},{13,9},{1,13},{6,2},{10,6},{... | collective-permute-start | bytes 12296 | tf_op jit(solution)/shard_map/ppermute | solution.py:25
  151.8 19.2 %collective-permute-start.27 = (f32[2,4,1,128]{3,2,1,0:T(1,128)}, f32[2,4,1,128]{3,2,1,0:T(1,128)}, u32[]{:S(2)}, u32[]{:S(2)}) collective-permute-start(f32[2,4,1,128]{3,2,1,0:T(1,128)} %get-tuple-element.130), channel_id=1, source_target_pairs={{0,4},{4,8},{8,12},{12,0},{1,5},{5,9},{9,13},{13,1},{2,6},{6,10},{... | collective-permute-start | bytes 12296 | tf_op jit(solution)/shard_map/ppermute | solution.py:24
  154.3 17.8 %collective-permute-start.28 = (f32[2,1,8,128]{3,2,1,0:T(8,128)}, f32[2,1,8,128]{3,2,1,0:T(8,128)}, u32[]{:S(2)}, u32[]{:S(2)}) collective-permute-start(f32[2,1,8,128]{3,2,1,0:T(8,128)} %get-tuple-element.133), channel_id=1, source_target_pairs={{16,0},{32,16},{48,32},{64,48},{80,64},{96,80},{112,96},{128,112},... | collective-permute-start | bytes 24584 | tf_op jit(solution)/shard_map/ppermute | solution.py:25
  192.5 19.4 %collective-permute-start.32 = (f32[2,4,1,128]{3,2,1,0:T(1,128)S(1)}, f32[2,4,1,128]{3,2,1,0:T(1,128)S(1)}, u32[]{:S(2)}, u32[]{:S(2)}) collective-permute-start(f32[2,4,1,128]{3,2,1,0:T(1,128)S(1)} %get-tuple-element.117), channel_id=1, source_target_pairs={{4,0},{8,4},{12,8},{0,12},{5,1},{9,5},{13,9},{1,13},{6,2},{10,6},{... | collective-permute-start | bytes 12296 | tf_op jit(solution)/shard_map/ppermute | solution.py:25
  197.4 14.6 %collective-permute-start.33 = (f32[2,4,1,128]{3,2,1,0:T(1,128)S(1)}, f32[2,4,1,128]{3,2,1,0:T(1,128)S(1)}, u32[]{:S(2)}, u32[]{:S(2)}) collective-permute-start(f32[2,4,1,128]{3,2,1,0:T(1,128)S(1)} %get-tuple-element.118), channel_id=1, source_target_pairs={{0,4},{4,8},{8,12},{12,0},{1,5},{5,9},{9,13},{13,1},{2,6},{6,10},{... | collective-permute-start | bytes 12296 | tf_op jit(solution)/shard_map/ppermute | solution.py:24
  230.2 18.9 %collective-permute-start.38 = (f32[2,4,1,128]{3,2,1,0:T(1,128)S(1)}, f32[2,4,1,128]{3,2,1,0:T(1,128)S(1)}, u32[]{:S(2)}, u32[]{:S(2)}) collective-permute-start(f32[2,4,1,128]{3,2,1,0:T(1,128)S(1)} %get-tuple-element.105), channel_id=1, source_target_pairs={{4,0},{8,4},{12,8},{0,12},{5,1},{9,5},{13,9},{1,13},{6,2},{10,6},{... | collective-permute-start | bytes 12296 | tf_op jit(solution)/shard_map/ppermute | solution.py:25
  234.8 14.4 %collective-permute-start.39 = (f32[2,4,1,128]{3,2,1,0:T(1,128)S(1)}, f32[2,4,1,128]{3,2,1,0:T(1,128)S(1)}, u32[]{:S(2)}, u32[]{:S(2)}) collective-permute-start(f32[2,4,1,128]{3,2,1,0:T(1,128)S(1)} %get-tuple-element.106), channel_id=1, source_target_pairs={{0,4},{4,8},{8,12},{12,0},{1,5},{5,9},{9,13},{13,1},{2,6},{6,10},{... | collective-permute-start | bytes 12296 | tf_op jit(solution)/shard_map/ppermute | solution.py:24
  267.7 18.9 %collective-permute-start.44 = (f32[2,4,1,128]{3,2,1,0:T(1,128)S(1)}, f32[2,4,1,128]{3,2,1,0:T(1,128)S(1)}, u32[]{:S(2)}, u32[]{:S(2)}) collective-permute-start(f32[2,4,1,128]{3,2,1,0:T(1,128)S(1)} %get-tuple-element.93), channel_id=1, source_target_pairs={{4,0},{8,4},{12,8},{0,12},{5,1},{9,5},{13,9},{1,13},{6,2},{10,6},{... | collective-permute-start | bytes 12296 | tf_op jit(solution)/shard_map/ppermute | solution.py:25
  272.3 14.4 %collective-permute-start.45 = (f32[2,4,1,128]{3,2,1,0:T(1,128)S(1)}, f32[2,4,1,128]{3,2,1,0:T(1,128)S(1)}, u32[]{:S(2)}, u32[]{:S(2)}) collective-permute-start(f32[2,4,1,128]{3,2,1,0:T(1,128)S(1)} %get-tuple-element.94), channel_id=1, source_target_pairs={{0,4},{4,8},{8,12},{12,0},{1,5},{5,9},{9,13},{13,1},{2,6},{6,10},{... | collective-permute-start | bytes 12296 | tf_op jit(solution)/shard_map/ppermute | solution.py:24
  (203 other events, 3013.5 us)
Sparse Core Ops, SparseCore 0:
  303.5 500.5 all-reduce.2
